TPU v7x, 32 devices: a whole 2x2x4 slice. The times are simulated.
32 devices in a mesh: group: 16 (over z, x, core), head: 2 (over y).
Axes of the slice: x: 2, y: 2, z: 4, core: 2. Of those that a mesh axis runs over, the one named last changes fastest.
Arguments:
- query: bfloat16 [16, 512, 5120], P('group', None, 'head'), may hold values from -1.7265625 to 1.7265625
- key: bfloat16 [16, 512, 5120], P('group', None, 'head'), may hold values from -1.7265625 to 1.7265625
- value: bfloat16 [16, 512, 5120], P('group', None, 'head'), may hold values from -6 to 6
- output: bfloat16 [16, 512, 5120], P('group', None, 'head'), may hold values from -1.5 to 1.5
- grad_out: bfloat16 [16, 512, 5120], P('group', 'head'), may hold values from -169 to 169
- log_sum: float32 [16, 40, 512], P('group', 'head'), as said below
- group_length: int32 [16], replicated, may hold values from 256 to 512, as said below
- cache_source: int32 [16], replicated, may hold values from -1 to 14, as said below
Outputs:
- grad_query: bfloat16 [16, 512, 5120], P('group', 'head')
- grad_key: bfloat16 [16, 512, 5120], P('group', 'head')
- grad_value: bfloat16 [16, 512, 5120], P('group', 'head')
Inputs may be any that keep to these rules, and one draw needn't show every extreme that they name: group_length[c] counts the first, live token slots of group c; some group is full. cache_source[c] is c - 1 where group c attends the preceding group's cache and -1 where a rollout starts; it is -1 for group 0 and c - 1 for the last group. `log_sum`: each entry lies between ln(512) + 0.2 and ln(1024) + 0.8.
All inputs are finite; a program needn't handle non-finite values.
Results may differ from a plain program's by a relative error of at most 0.0049.
Values may be sent and summed in bfloat16 or wider, within the bound.
No kernel may reach another device: no remote copies, remote signals or barrier semaphores. Data moves between devices by JAX's collectives and lax.ppermute only.
A program may use at most 128 MiB of HBM per device.

v0:
```python
import functools
import math

import jax
import jax.numpy as jnp
from jax import lax
from jax.experimental import pallas as pl
from jax.experimental.pallas import tpu as pltpu
from jax.sharding import PartitionSpec as P


HEAD_DIM = 128
STAT_ROWS = 24
DEAD = 1e30
LOG2E = 1.4426950408889634
VMEM_LIMIT = 30 * 1024 * 1024
KEY_TILE = 512
CHUNKS = (4, 4, 4, 4, 4)
MOVES = ((0,),)
GROUPS = ((0, 1), (2, 3, 4))


def shifted(block, axis, distance):
    size = lax.axis_size(axis)
    return lax.ppermute(block, axis, [(i, (i + distance) % size) for i in range(size)])


def passed_along(block, axis, distance):
    devices = range(lax.axis_size(axis))
    route = [(i - distance, i) for i in devices if i - distance in devices]
    return lax.ppermute(block, axis, route)


def chunks_of(head_count):
    if head_count == sum(CHUNKS):
        return CHUNKS
    count = min(head_count, len(CHUNKS))
    return tuple((head_count * (i + 1)) // count - (head_count * i) // count for i in range(count))


def within(groups, chunks):
    groups = [tuple(i for i in group if i < chunks) for group in groups]
    return [group for group in groups if group]


def three_parts(x):
    high = x.astype(jnp.bfloat16)
    rest = x - high.astype(jnp.float32)
    mid = rest.astype(jnp.bfloat16)
    low = (rest - mid.astype(jnp.float32)).astype(jnp.bfloat16)
    return high, mid, low


def cut_kernel(grad, *refs, plan, heads):
    outs, sems = refs[:-1], refs[-1]
    size = grad.shape[1] // (heads * HEAD_DIM)
    copies = []
    for i, (out, (rel, first)) in enumerate(zip(outs, plan)):
        peer = lax.rem(lax.axis_index("head") + rel, size)
        column = pl.multiple_of((peer * heads + first) * HEAD_DIM, HEAD_DIM)
        copies.append(
            pltpu.make_async_copy(grad.at[:, pl.ds(column, out.shape[1])], out, sems.at[i])
        )
    for copy in copies:
        copy.start()
    for copy in copies:
        copy.wait()


def cut(grad, heads, plan, counts):
    shapes = [(grad.shape[0], count * HEAD_DIM) for count in counts]
    return pl.pallas_call(
        functools.partial(cut_kernel, plan=plan, heads=heads),
        grid=(1,),
        in_specs=[pl.BlockSpec(memory_space=pl.ANY)],
        out_specs=[pl.BlockSpec(shape, lambda i: (0, 0)) for shape in shapes],
        out_shape=[jax.ShapeDtypeStruct(shape, jnp.bfloat16) for shape in shapes],
        scratch_shapes=[pltpu.SemaphoreType.DMA((len(plan),))],
        compiler_params=pltpu.CompilerParams(vmem_limit_bytes=VMEM_LIMIT),
        cost_estimate=pl.CostEstimate(
            flops=0,
            bytes_accessed=sum(4 * math.prod(shape) for shape in shapes),
            transcendentals=0,
        ),
        name="cut",
    )(grad)


def pack_kernel(grad, grad_recv, out, lse, *refs, first, joined):
    me = lax.axis_index("head")
    query, packed, scratch, sems = refs[0], refs[joined], refs[joined + 1 : -1], refs[-1]
    grad_own, out_own = scratch[:2]
    count, height, _ = packed.shape
    rows = out.shape[0]
    top = height - rows - STAT_ROWS
    per = grad.shape[0]
    size = rows // per
    lanes = rows // HEAD_DIM
    width = count * HEAD_DIM
    heads = out.shape[1] // HEAD_DIM
    column = pl.multiple_of((me * heads + first) * HEAD_DIM, HEAD_DIM)
    copies = [
        pltpu.make_async_copy(grad.at[:, pl.ds(column, width)], grad_own, sems.at[0]),
        pltpu.make_async_copy(out.at[:, pl.ds(first * HEAD_DIM, width)], out_own, sems.at[1]),
    ]
    if top:
        copies.append(
            pltpu.make_async_copy(
                query.at[:, pl.ds(first * HEAD_DIM, width)], scratch[2], sems.at[2]
            )
        )
    for copy in copies:
        copy.start()
    for copy in copies:
        copy.wait()
    ones = jnp.ones((16, HEAD_DIM), jnp.bfloat16)
    for h in range(count):
        cols = slice(h * HEAD_DIM, (h + 1) * HEAD_DIM)
        for r in range(size):
            start = pl.multiple_of(lax.rem(me - r + size, size) * per, per)
            block = grad_own[:, cols] if r == 0 else grad_recv[r - 1, :, cols]
            packed[h, pl.ds(pl.multiple_of(top + start, per), per), :] = block
        if top:
            packed[h, :top, :] = scratch[2][:, cols]
        product = packed[h, top : top + rows].astype(jnp.float32) * out_own[:, cols].astype(jnp.float32)
        delta = sum(
            lax.dot_general(
                ones, part, (((1,), (1,)), ((), ())), preferred_element_type=jnp.float32
            )
            for part in three_parts(product)
        )[:1]
        log_sum = lse[first + h] * LOG2E
        parts = three_parts(delta) + three_parts(log_sum)
        pieces = [
            part[:, j * HEAD_DIM : (j + 1) * HEAD_DIM].astype(jnp.float32)
            for part in parts
            for j in range(lanes)
        ]
        if len(pieces) < STAT_ROWS:
            pieces.append(jnp.zeros((STAT_ROWS - len(pieces), HEAD_DIM), jnp.float32))
        packed[h, top + rows :, :] = jnp.concatenate(pieces, axis=0).astype(jnp.bfloat16)


def pack(grad, grad_recv, out, lse, query, first, count, joined):
    rows = out.shape[0]
    per = grad.shape[0]
    height = rows * (1 + joined) + STAT_ROWS
    width = count * HEAD_DIM
    any_spec = pl.BlockSpec(memory_space=pltpu.HBM if first == 0 else pl.ANY)
    return pl.pallas_call(
        functools.partial(pack_kernel, first=first, joined=joined),
        grid_spec=pltpu.PrefetchScalarGridSpec(
            num_scalar_prefetch=0,
            grid=(1,),
            in_specs=[
                any_spec,
                pl.BlockSpec(grad_recv.shape, lambda i: (0, 0, 0)),
                any_spec,
                pl.BlockSpec(lse.shape, lambda i: (0, 0, 0)),
            ]
            + [any_spec] * joined,
            out_specs=pl.BlockSpec((count, height, HEAD_DIM), lambda i: (0, 0, 0)),
            scratch_shapes=[
                pltpu.VMEM((per, width), jnp.bfloat16),
                pltpu.VMEM((rows, width), jnp.bfloat16),
            ]
            + [pltpu.VMEM((rows, width), jnp.bfloat16)] * joined
            + [pltpu.SemaphoreType.DMA((2 + joined,))],
        ),
        out_shape=jax.ShapeDtypeStruct((count, height, HEAD_DIM), jnp.bfloat16),
        compiler_params=pltpu.CompilerParams(vmem_limit_bytes=VMEM_LIMIT),
        cost_estimate=pl.CostEstimate(
            flops=count * rows * HEAD_DIM * 16,
            bytes_accessed=count * rows * HEAD_DIM * 6,
            transcendentals=0,
        ),
        name="pack",
    )(grad, grad_recv, out, lse, *[query] * joined)


def stat_row(stats, at, lanes):
    total = (
        stats[at : at + lanes] + stats[at + lanes : at + 2 * lanes]
    ) + stats[at + 2 * lanes : at + 3 * lanes]
    return jnp.concatenate([total[j : j + 1] for j in range(lanes)], axis=1)


def stat_rows(packed, at, rows, query_len):
    lanes = rows // HEAD_DIM
    stats = packed[at, packed.shape[1] - STAT_ROWS :, :].astype(jnp.float32)
    alive = lax.broadcasted_iota(jnp.int32, (1, rows), 1) < query_len
    log_sum = jnp.where(alive, stat_row(stats, 3 * lanes, lanes), DEAD)
    return stat_row(stats, 0, lanes), log_sum


def head_grads(key, value, queries, grad, stats, own_len, both, tile):
    rows = key.shape[0]
    scale = HEAD_DIM**-0.5
    across = (((1,), (1,)), ((), ()))
    live_t = lax.broadcasted_iota(jnp.int32, (1, rows), 1) < own_len
    key_t = jnp.where(live_t, key[...].astype(jnp.float32).T, 0.0).astype(jnp.bfloat16)
    all_queries, all_grad = jnp.concatenate(queries, axis=0), jnp.concatenate(grad, axis=0)
    dq_t = None
    for at in range(0, rows, tile):
        k, v = key[at : at + tile, :], value[at : at + tile, :]
        probs, grad_scores = [], []
        for i, (delta, log_sum) in enumerate(stats):
            scores = lax.dot_general(k, queries[i], across, preferred_element_type=jnp.float32)
            prob = jnp.exp2(scores * (scale * LOG2E) - log_sum)
            grad_prob = lax.dot_general(v, grad[i], across, preferred_element_type=jnp.float32)
            grad_scores.append((prob * (grad_prob - delta)).astype(jnp.bfloat16))
            probs.append(prob.astype(jnp.bfloat16))
        probs = jnp.concatenate(probs, axis=1)
        grad_scores = jnp.concatenate(grad_scores, axis=1)
        dv = jnp.dot(probs, all_grad, preferred_element_type=jnp.float32)
        dk = jnp.dot(grad_scores, all_queries, preferred_element_type=jnp.float32)
        live = lax.broadcasted_iota(jnp.int32, (tile, 1), 0) + at < own_len
        both[0, at : at + tile, :] = jnp.where(live, dk * scale, 0.0).astype(jnp.bfloat16)
        both[1, at : at + tile, :] = jnp.where(live, dv, 0.0).astype(jnp.bfloat16)
        part = jnp.dot(
            key_t[:, at : at + tile], grad_scores, preferred_element_type=jnp.float32
        )
        dq_t = part if dq_t is None else dq_t + part
    return dq_t


def grads_kernel(lengths, sources, *refs, carried, tile):
    key, value, query, own, next_query, following = refs[:6]
    refs = refs[6 + carried :]
    key_out, value_out, send, query_own, query_cross, both = refs
    me, group_at = lax.axis_index("head"), lax.axis_index("group")
    own_len = lengths[group_at]
    after = lax.min(group_at + 1, lengths.shape[0] - 1)
    linked = (group_at + 1 == after) & (sources[after] == group_at)
    cross_len = jnp.where(linked, lengths[after], 0)
    rows = key.shape[0]
    per = key_out.shape[0]
    size = rows // per
    for p in range(query_own.shape[0]):
        cols = slice(p * HEAD_DIM, (p + 1) * HEAD_DIM)
        top = own.shape[1] - rows - STAT_ROWS
        queries = (query[:, cols], following[p, :rows, :] if top else next_query[:, cols])
        stats = (stat_rows(own, p, rows, own_len), stat_rows(following, p, rows, cross_len))
        grad = (own[p, top : top + rows, :], following[p, top : top + rows, :])
        dq_t = head_grads(
            key.at[:, cols], value.at[:, cols], queries, grad, stats, own_len, both.at[:, :, cols], tile
        )
        query_own[p] = dq_t[:, :rows].T * HEAD_DIM**-0.5
        query_cross[p] = (dq_t[:, rows:].T * HEAD_DIM**-0.5).astype(jnp.bfloat16)
    for r in range(size):
        start = pl.multiple_of(lax.rem(me - r + size, size) * per, per)
        if r == 0:
            key_out[...] = both[0, pl.ds(start, per), :]
            value_out[...] = both[1, pl.ds(start, per), :]
        else:
            send[r - 1, 0] = both[0, pl.ds(start, per), :]
            send[r - 1, 1] = both[1, pl.ds(start, per), :]


def grads(
    lengths, sources, key, value, query, own, next_query, next_first, following, carried, aliases,
    size, first, count, base, total,
):
    rows, width = key.shape
    per = rows // size
    heads = width // HEAD_DIM
    step = 2 if not any(n % 2 for n in (heads, first, count, base, next_first)) else 1
    wide = step * HEAD_DIM
    height = own.shape[1]
    any_spec = pl.BlockSpec(memory_space=pl.ANY)
    own_spec = pl.BlockSpec(
        (per, wide), lambda h, *_: (0, (lax.axis_index("head") * heads + first) // step + h)
    )
    full = jax.ShapeDtypeStruct((per, width * size), jnp.bfloat16)
    return pl.pallas_call(
        functools.partial(grads_kernel, carried=len(carried), tile=min(KEY_TILE, rows)),
        grid_spec=pltpu.PrefetchScalarGridSpec(
            num_scalar_prefetch=2,
            grid=(count // step,),
            in_specs=[
                pl.BlockSpec((rows, wide), lambda h, *_: (0, first // step + h)),
                pl.BlockSpec((rows, wide), lambda h, *_: (0, first // step + h)),
                pl.BlockSpec((rows, wide), lambda h, *_: (0, first // step + h)),
                pl.BlockSpec((step, height, HEAD_DIM), lambda h, *_: (h, 0, 0)),
                pl.BlockSpec((rows, wide), lambda h, *_: (0, (first - next_first) // step + h))
                if height == rows + STAT_ROWS
                else any_spec,
                pl.BlockSpec((step, height, HEAD_DIM), lambda h, *_: (h, 0, 0)),
            ]
            + [any_spec] * len(carried),
            out_specs=[
                own_spec,
                own_spec,
                pl.BlockSpec((size - 1, 2, per, wide), lambda h, *_: (0, 0, 0, h)),
                pl.BlockSpec((step, rows, HEAD_DIM), lambda h, *_: (base // step + h, 0, 0)),
                pl.BlockSpec((step, rows, HEAD_DIM), lambda h, *_: (base // step + h, 0, 0)),
            ],
            scratch_shapes=[pltpu.VMEM((2, rows, wide), jnp.bfloat16)],
        ),
        out_shape=[
            full,
            full,
            jax.ShapeDtypeStruct((size - 1, 2, per, count * HEAD_DIM), jnp.bfloat16),
            jax.ShapeDtypeStruct((total, rows, HEAD_DIM), jnp.float32),
            jax.ShapeDtypeStruct((total, rows, HEAD_DIM), jnp.bfloat16),
        ],
        input_output_aliases={8 + i: out for i, out in enumerate(aliases)},
        compiler_params=pltpu.CompilerParams(vmem_limit_bytes=VMEM_LIMIT),
        cost_estimate=pl.CostEstimate(
            flops=count * 20 * rows * rows * HEAD_DIM,
            bytes_accessed=count * rows * HEAD_DIM * 24,
            transcendentals=count * 2 * rows * rows,
        ),
        name="grads",
    )(lengths, sources, key, value, query, own, next_query, following, *carried)


def query_kernel(own, back, *refs, carried, first, heads):
    query_out, send, total, sem = refs[carried:]
    me = lax.axis_index("head")
    count, rows, _ = own.shape
    per = query_out.shape[0]
    size = rows // per
    for h in range(count):
        cols = slice(h * HEAD_DIM, (h + 1) * HEAD_DIM)
        total[:, cols] = (own[h] + back[h].astype(jnp.float32)).astype(jnp.bfloat16)
    column = pl.multiple_of((me * heads + first) * HEAD_DIM, HEAD_DIM)
    start = pl.multiple_of(me * per, per)
    copy = pltpu.make_async_copy(
        total.at[pl.ds(start, per), :],
        query_out.at[:, pl.ds(column, count * HEAD_DIM)],
        sem.at[0],
    )
    copy.start()
    for r in range(1, size):
        start = pl.multiple_of(lax.rem(me - r + size, size) * per, per)
        send[r - 1] = total[pl.ds(start, per), :]
    copy.wait()


def query_sum(own, back, carried, size, heads, first):
    count, rows, _ = own.shape
    per = rows // size
    any_spec = pl.BlockSpec(memory_space=pl.ANY)
    whole = (count, rows, HEAD_DIM)
    return pl.pallas_call(
        functools.partial(query_kernel, carried=len(carried), first=first, heads=heads),
        grid_spec=pltpu.PrefetchScalarGridSpec(
            num_scalar_prefetch=0,
            grid=(1,),
            in_specs=[
                pl.BlockSpec(whole, lambda i: (0, 0, 0)),
                pl.BlockSpec(whole, lambda i: (0, 0, 0)),
            ]
            + [any_spec] * len(carried),
            out_specs=[
                any_spec,
                pl.BlockSpec((size - 1, per, count * HEAD_DIM), lambda i: (0, 0, 0)),
            ],
            scratch_shapes=[
                pltpu.VMEM((rows, count * HEAD_DIM), jnp.bfloat16),
                pltpu.SemaphoreType.DMA((1,)),
            ],
        ),
        out_shape=[
            jax.ShapeDtypeStruct((per, heads * size * HEAD_DIM), jnp.bfloat16),
            jax.ShapeDtypeStruct((size - 1, per, count * HEAD_DIM), jnp.bfloat16),
        ],
        input_output_aliases={2 + i: i for i in range(len(carried))},
        compiler_params=pltpu.CompilerParams(vmem_limit_bytes=VMEM_LIMIT),
        cost_estimate=pl.CostEstimate(
            flops=count * rows * HEAD_DIM,
            bytes_accessed=count * rows * HEAD_DIM * 8,
            transcendentals=0,
        ),
        name="query_sum",
    )(own, back, *carried)


def place_kernel(*refs, plan, targets, size, heads):
    blocks = refs[: len(plan)]
    outs = refs[len(plan) + targets : len(plan) + 2 * targets]
    sems = refs[-1]
    me = lax.axis_index("head")
    copies = []
    for block, (rel, first, dests) in zip(blocks, plan):
        peer = lax.rem(me + rel, size)
        width = block.shape[-1]
        column = pl.multiple_of((peer * heads + first) * HEAD_DIM, HEAD_DIM)
        for j, dest in enumerate(dests):
            copies.append(
                pltpu.make_async_copy(
                    block.at[j], outs[dest].at[:, pl.ds(column, width)], sems.at[len(copies)]
                )
            )
    for copy in copies:
        copy.start()
    for copy in copies:
        copy.wait()


def place(blocks, plan, outs, size, heads):
    any_spec = pl.BlockSpec(memory_space=pl.ANY)
    copies = sum(len(dests) for _, _, dests in plan)
    return pl.pallas_call(
        functools.partial(
            place_kernel, plan=plan, targets=len(outs), size=size, heads=heads
        ),
        grid_spec=pltpu.PrefetchScalarGridSpec(
            num_scalar_prefetch=0,
            grid=(1,),
            in_specs=[
                any_spec
                for _ in (*blocks, *outs)
            ],
            out_specs=[any_spec] * len(outs),
            scratch_shapes=[pltpu.SemaphoreType.DMA((copies,))],
        ),
        out_shape=[jax.ShapeDtypeStruct(o.shape, o.dtype) for o in outs],
        input_output_aliases={len(blocks) + i: i for i in range(len(outs))},
        compiler_params=pltpu.CompilerParams(vmem_limit_bytes=VMEM_LIMIT),
        cost_estimate=pl.CostEstimate(
            flops=0,
            bytes_accessed=sum(4 * math.prod(b.shape) for b in blocks),
            transcendentals=0,
        ),
        name="place",
    )(*blocks, *outs)


def on_device(query, key, value, output, grad_out, log_sum, group_length, cache_source):
    size = lax.axis_size("head")
    me = lax.axis_index("head")
    query, key, value, output = query[0], key[0], value[0], output[0]
    grad, lse = grad_out[0], log_sum[0][:, None, :]
    width = query.shape[1]
    heads = width // HEAD_DIM
    counts = chunks_of(heads)
    firsts = [sum(counts[:i]) for i in range(len(counts))]

    rels = range(1, size)
    moves = within(MOVES, len(counts))
    plan = [(rel, firsts[i]) for i in range(1, len(counts)) for rel in rels]
    widths = [counts[i] for i in range(1, len(counts)) for rel in rels]
    pieces = cut(grad, heads, tuple(plan), widths)
    pieces = list(pieces)
    for rel in reversed(rels):
        start = (lax.rem(me + rel, size) * heads + firsts[0]) * HEAD_DIM
        block = lax.dynamic_slice_in_dim(grad, start, counts[0] * HEAD_DIM, axis=1)
        pieces = [block] + pieces

    received = []
    for i in range(len(counts)):
        blocks = []
        for rel in rels:
            blocks.append(shifted(pieces[i * (size - 1) + rel - 1], "head", rel)[None])
        received.append(blocks[0] if size == 2 else jnp.concatenate(blocks, axis=0))

    next_queries = {}
    for group in moves:
        start, end = firsts[group[0]], firsts[group[-1]] + counts[group[-1]]
        block = query[:, start * HEAD_DIM : end * HEAD_DIM]
        moved = passed_along(block, "group", -1)
        for i in group:
            next_queries[i] = (moved, firsts[group[0]])

    packs, nexts = [], []
    for i, (first, count) in enumerate(zip(firsts, counts)):
        joined = int(i not in next_queries)
        packs.append(pack(grad, received[i], output, lse, query, first, count, joined))
        nexts.append(passed_along(packs[i], "group", -1))

    kv_outs, q_outs = (), ()
    kv_blocks, kv_plan, q_blocks, q_plan = [], [], [], []
    for group in within(GROUPS, len(counts)):
        total = sum(counts[i] for i in group)
        base, q_parts = 0, ()
        for i in group:
            aliases = ((0, 1) if kv_outs else ()) + ((3, 4) if q_parts else ())
            key_out, value_out, kv_send, q_own, q_cross = grads(
                group_length, cache_source, key, value, query, packs[i], *next_queries.get(i, (query, 0)), nexts[i],
                kv_outs + q_parts, aliases, size, firsts[i], counts[i], base, total,
            )
            kv_outs, q_parts = (key_out, value_out), (q_own, q_cross)
            base += counts[i]
            for rel in range(1, size):
                kv_blocks.append(shifted(kv_send[rel - 1], "head", -rel))
                kv_plan.append((rel, firsts[i], (0, 1)))
        back = passed_along(q_cross, "group", 1)
        first = firsts[group[0]]
        query_out, q_send = query_sum(q_own, back, q_outs, size, heads, first)
        q_outs = (query_out,)
        for rel in range(1, size):
            q_blocks.append(shifted(q_send[rel - 1][None], "head", -rel))
            q_plan.append((rel, first, (0,)))

    last = size - 1
    key_out, value_out = place(kv_blocks, tuple(kv_plan), kv_outs, size, heads)
    (query_out,) = place(q_blocks[:-last], tuple(q_plan[:-last]), q_outs, size, heads)
    (query_out,) = place(
        q_blocks[-last:], tuple(q_plan[-last:]), (query_out,), size, heads
    )
    return query_out[None], key_out[None], value_out[None]


def solution(mesh):
    in_specs = (
        P("group", None, "head"),
        P("group", None, "head"),
        P("group", None, "head"),
        P("group", None, "head"),
        P("group", "head", None),
        P("group", "head", None),
        P(),
        P(),
    )
    out_specs = (P("group", "head", None), P("group", "head", None), P("group", "head", None))

    return jax.shard_map(
        on_device, mesh=mesh, in_specs=in_specs, out_specs=out_specs, check_vma=False
    )
```

profile of v0, /device:TPU:6, one launch (start us, length us, event | category | flops | bytes accessed | tf_op | source)
XLA Modules:
  0.0 193.0 jit_solution(311679856016955907)
XLA Ops:
  0.7 1.9 copy-done.1
  2.5 0.9 cut.1
  3.5 0.7 copy-done.9
  4.2 0.5 collective-permute-start.6
  4.7 1.5 collective-permute-start.4
  6.2 1.0 dynamic-slice_bitcast_fusion
  7.1 0.6 collective-permute-start.8
  7.7 5.8 %collective-permute-done.6 = bf16[256,512]{1,0:T(8,128)(2,1)S(1)} collective-permute-done((bf16[256,512]{1,0:T(8,128)(2,1)}, bf16[256,512]{1,0:T(8,128)(2,1)S(1)}, u32[]{:S(2)}, u32[]{:S(2)}) %collective-permute-start.6) | collective-permute-done | bytes 262176 | tf_op jit(solution)/shard_map/ppermute | solution.py:25
  13.5 1.7 copy-done.2
  15.3 1.7 copy-done.3
  17.0 0.8 pack.8.refs_3_
  17.9 1.9 collective-permute-start.7
  19.8 0.6 collective-permute-start.2
  20.4 2.1 %collective-permute-start.9 = (bf16[512,512]{1,0:T(8,128)(2,1)S(1)}, bf16[512,512]{1,0:T(8,128)(2,1)S(1)}, u32[]{:S(2)}, u32[]{:S(2)}) collective-permute-start(bf16[512,512]{1,0:T(8,128)(2,1)S(1)} %slice.4), channel_id=1, source_target_pairs={{2,0},{4,2},{6,4},{8,6},{10,8},{12,10},{14,12},{16,14},{18,16},{20... | collective-permute-start | bytes 1572872 | tf_op jit(solution)/shard_map/ppermute | solution.py:31
  22.5 1.8 collective-permute-start
  24.3 0.8 pack.7.refs_3_
  25.2 1.9 collective-permute-start.5
  27.1 1.1 pack.9.refs_3_
  28.2 1.8 collective-permute-done.2
  29.9 1.9 collective-permute-start.10
  31.8 0.8 pack.6.refs_3_
  32.7 2.2 %collective-permute-done = bf16[256,512]{1,0:T(8,128)(2,1)S(1)} collective-permute-done((bf16[256,512]{1,0:T(8,128)(2,1)S(1)}, bf16[256,512]{1,0:T(8,128)(2,1)S(1)}, u32[]{:S(2)}, u32[]{:S(2)}) %collective-permute-start) | collective-permute-done | bytes 262176 | tf_op jit(solution)/shard_map/ppermute | solution.py:25
  34.9 1.9 collective-permute-start.3
  36.8 0.8 pack.5.refs_3_
  38.0 4.0 %collective-permute-start.1 = (bf16[4,1048,128]{2,1,0:T(8,128)(2,1)S(1)}, bf16[4,1048,128]{2,1,0:T(8,128)(2,1)S(1)}, u32[]{:S(2)}, u32[]{:S(2)}) collective-permute-start(bf16[4,1048,128]{2,1,0:T(8,128)(2,1)S(1)} %pack.5.refs_3_), channel_id=1, source_target_pairs={{2,0},{4,2},{6,4},{8,6},{10,8},{12,10},{14,12},{16,14},{18,16},{20... | collective-permute-start | bytes 3219464 | tf_op jit(solution)/shard_map/ppermute | solution.py:31
  42.0 13.4 %collective-permute-done.10.refs_5_ = bf16[4,536,128]{2,1,0:T(8,128)(2,1)S(1)} collective-permute-done((bf16[4,536,128]{2,1,0:T(8,128)(2,1)S(1)}, bf16[4,536,128]{2,1,0:T(8,128)(2,1)S(1)}, u32[]{:S(2)}, u32[]{:S(2)}) %collective-permute-start.10) | collective-permute-done | bytes 548896 | tf_op jit(solution)/shard_map/ppermute | solution.py:31
  55.4 7.2 %grads.5 = (bf16[256,5120]{1,0:T(8,128)(2,1)}, bf16[256,5120]{1,0:T(8,128)(2,1)}, bf16[1,2,256,512]{3,2,1,0:T(8,128)(2,1)S(1)}, f32[8,512,128]{2,1,0:T(8,128)S(1)}, bf16[8,512,128]{2,1,0:T(8,128)(2,1)S(1)}) custom-call(s32[16]{0:T(128)S(1)} %copy-done.7, s32[16]{0:T(128)S(1)} %copy-done.8, bf16[512,2560]{1,0:T(8,128)(2,1)S(1)} %bitcast.46, ...), custom_call_target="tpu_custom_call" | custom-call | flops 2684354560 | bytes 6291456 | tf_op jit(solution)/shard_map/grads/pallas_call | solution.py:275
  62.6 7.2 %grads.6 = (bf16[256,5120]{1,0:T(8,128)(2,1)}, bf16[256,5120]{1,0:T(8,128)(2,1)}, bf16[1,2,256,512]{3,2,1,0:T(8,128)(2,1)S(1)}, f32[8,512,128]{2,1,0:T(8,128)S(1)}, bf16[8,512,128]{2,1,0:T(8,128)(2,1)S(1)}) custom-call(s32[16]{0:T(128)S(1)} %copy-done.7, s32[16]{0:T(128)S(1)} %copy-done.8, ...), custom_call_target="tpu_custom_call", output_to_operand_aliasing={{0}: (8, {}), {1}: (9, {}), {3}: (10, {}), {4}: (11, {})} | custom-call | flops 2684354560 | bytes 6291456 | tf_op jit(solution)/shard_map/grads/pallas_call | solution.py:275
  69.8 7.2 %grads.7 = (bf16[256,5120]{1,0:T(8,128)(2,1)}, bf16[256,5120]{1,0:T(8,128)(2,1)}, bf16[1,2,256,512]{3,2,1,0:T(8,128)(2,1)S(1)}, f32[12,512,128]{2,1,0:T(8,128)S(1)}, bf16[12,512,128]{2,1,0:T(8,128)(2,1)S(1)}) custom-call(s32[16]{0:T(128)S(1)} %copy-done.7, s32[16]{0:T(128)S(1)} %copy-done.8, ...), custom_call_target="tpu_custom_call", output_to_operand_aliasing={{0}: (8, {}), {1}: (9, {})} | custom-call | flops 2684354560 | bytes 6291456 | tf_op jit(solution)/shard_map/grads/pallas_call | solution.py:275
  77.0 7.2 %grads.8 = (bf16[256,5120]{1,0:T(8,128)(2,1)}, bf16[256,5120]{1,0:T(8,128)(2,1)}, bf16[1,2,256,512]{3,2,1,0:T(8,128)(2,1)S(1)}, f32[12,512,128]{2,1,0:T(8,128)S(1)}, bf16[12,512,128]{2,1,0:T(8,128)(2,1)S(1)}) custom-call(s32[16]{0:T(128)S(1)} %copy-done.7, ...), custom_call_target="tpu_custom_call", output_to_operand_aliasing={{0}: (8, {}), {1}: (9, {}), {3}: (10, {}), {4}: (11, {})} | custom-call | flops 2684354560 | bytes 6291456 | tf_op jit(solution)/shard_map/grads/pallas_call | solution.py:275
  84.2 7.4 %grads.9 = (bf16[256,5120]{1,0:T(8,128)(2,1)}, bf16[256,5120]{1,0:T(8,128)(2,1)}, bf16[1,2,256,512]{3,2,1,0:T(8,128)(2,1)S(1)}, f32[12,512,128]{2,1,0:T(8,128)S(1)}, bf16[12,512,128]{2,1,0:T(8,128)(2,1)S(1)}) custom-call(s32[16]{0:T(128)S(1)} %copy-done.7, ...), custom_call_target="tpu_custom_call", output_to_operand_aliasing={{0}: (8, {}), {1}: (9, {}), {3}: (10, {}), {4}: (11, {})} | custom-call | flops 2684354560 | bytes 6291456 | tf_op jit(solution)/shard_map/grads/pallas_call | solution.py:275
  91.6 3.7 %collective-permute-start.11 = (bf16[12,512,128]{2,1,0:T(8,128)(2,1)S(1)}, bf16[12,512,128]{2,1,0:T(8,128)(2,1)S(1)}, u32[]{:S(2)}, u32[]{:S(2)}) collective-permute-start(bf16[12,512,128]{2,1,0:T(8,128)(2,1)S(1)} %get-tuple-element.57), channel_id=1, source_target_pairs={{0,2},{2,4},{4,6},{6,8},{8,10},{10,12},{12,14},{14,16},{16,18},{18... | collective-permute-start | bytes 4718600 | tf_op jit(solution)/shard_map/ppermute | solution.py:31
  95.3 1.9 collective-permute-start.12
  97.3 0.6 collective-permute-start.15
  97.8 1.5 collective-permute-start.19
  99.4 25.4 %collective-permute-done.12.back = bf16[8,512,128]{2,1,0:T(8,128)(2,1)S(1)} collective-permute-done((bf16[8,512,128]{2,1,0:T(8,128)(2,1)S(1)}, bf16[8,512,128]{2,1,0:T(8,128)(2,1)S(1)}, u32[]{:S(2)}, u32[]{:S(2)}) %collective-permute-start.12) | collective-permute-done | bytes 1048608 | tf_op jit(solution)/shard_map/ppermute | solution.py:31
  124.7 1.3 query_sum.2
  126.0 1.4 query_sum.3
  127.4 0.6 collective-permute-start.13
  128.0 1.5 collective-permute-start.18
  130.0 1.5 collective-permute-start.16
  132.0 27.1 %collective-permute-done.18.refs_3_ = bf16[2,256,512]{2,1,0:T(8,128)(2,1)S(1)} collective-permute-done((bf16[2,256,512]{2,1,0:T(8,128)(2,1)S(1)}, bf16[2,256,512]{2,1,0:T(8,128)(2,1)S(1)}, u32[]{:S(2)}, u32[]{:S(2)}) %collective-permute-start.18) | collective-permute-done | bytes 524320 | tf_op jit(solution)/shard_map/ppermute | solution.py:25
  159.1 11.2 %collective-permute-done.17.refs_2_ = bf16[2,256,512]{2,1,0:T(8,128)(2,1)S(1)} collective-permute-done((bf16[2,256,512]{2,1,0:T(8,128)(2,1)S(1)}, bf16[2,256,512]{2,1,0:T(8,128)(2,1)S(1)}, u32[]{:S(2)}, u32[]{:S(2)}) %collective-permute-start.17) | collective-permute-done | bytes 524320 | tf_op jit(solution)/shard_map/ppermute | solution.py:25
  170.4 11.2 %collective-permute-done.16.refs_1_ = bf16[2,256,512]{2,1,0:T(8,128)(2,1)S(1)} collective-permute-done((bf16[2,256,512]{2,1,0:T(8,128)(2,1)S(1)}, bf16[2,256,512]{2,1,0:T(8,128)(2,1)S(1)}, u32[]{:S(2)}, u32[]{:S(2)}) %collective-permute-start.16) | collective-permute-done | bytes 524320 | tf_op jit(solution)/shard_map/ppermute | solution.py:25
  181.6 1.6 place.5
  183.2 7.9 %collective-permute-done.14.refs_0_ = bf16[1,256,1024]{2,1,0:T(8,128)(2,1)S(1)} collective-permute-done((bf16[1,256,1024]{2,1,0:T(8,128)(2,1)S(1)}, bf16[1,256,1024]{2,1,0:T(8,128)(2,1)S(1)}, u32[]{:S(2)}, u32[]{:S(2)}) %collective-permute-start.14) | collective-permute-done | bytes 524320 | tf_op jit(solution)/shard_map/ppermute | solution.py:25
  191.1 0.8 place.3.refs_1_
  191.9 0.9 place.4
  (32 shorter events, 1.4 us)
Async XLA Ops:
  0.6 12.9 %copy-start = (bf16[1,512,2560]{2,1,0:T(8,128)(2,1)S(1)}, bf16[1,512,2560]{2,1,0:T(8,128)(2,1)}, u32[]{:S(2)}) copy-start(bf16[1,512,2560]{2,1,0:T(8,128)(2,1)} %param.8) | copy-start | bytes 7864324
  0.6 1.9 copy-start.1
  2.5 11.0 %copy-start.6 = (f32[1,20,512]{2,0,1:T(1,128)S(1)}, f32[1,20,512]{2,0,1:T(1,128)}, u32[]{:S(2)}) copy-start(f32[1,20,512]{2,0,1:T(1,128)} %param.13) | copy-start | bytes 122884
  3.4 0.7 copy-start.9
  4.2 9.4 %collective-permute-start.6 = (bf16[256,512]{1,0:T(8,128)(2,1)}, bf16[256,512]{1,0:T(8,128)(2,1)S(1)}, u32[]{:S(2)}, u32[]{:S(2)}) collective-permute-start(bf16[256,512]{1,0:T(8,128)(2,1)} %get-tuple-element.41), channel_id=1, source_target_pairs={{0,1},{1,0},{2,3},{3,2},{4,5},{5,4},{6,7},{7,6},{8,9},{9,8},{10,11... | collective-permute-start | bytes 786440 | tf_op jit(solution)/shard_map/ppermute | solution.py:25
  4.7 17.8 %collective-permute-start.4 = (bf16[256,512]{1,0:T(8,128)(2,1)}, bf16[256,512]{1,0:T(8,128)(2,1)S(1)}, u32[]{:S(2)}, u32[]{:S(2)}) collective-permute-start(bf16[256,512]{1,0:T(8,128)(2,1)} %get-tuple-element.40), channel_id=1, source_target_pairs={{0,1},{1,0},{2,3},{3,2},{4,5},{5,4},{6,7},{7,6},{8,9},{9,8},{10,11... | collective-permute-start | bytes 786440 | tf_op jit(solution)/shard_map/ppermute | solution.py:25
  7.1 18.0 %collective-permute-start.8 = (bf16[256,512]{1,0:T(8,128)(2,1)S(1)}, bf16[256,512]{1,0:T(8,128)(2,1)S(1)}, u32[]{:S(2)}, u32[]{:S(2)}) collective-permute-start(bf16[256,512]{1,0:T(8,128)(2,1)S(1)} %dynamic-slice_bitcast_fusion), channel_id=1, source_target_pairs={{0,1},{1,0},{2,3},{3,2},{4,5},{5,4},{6,7},{7,6},{8,9},{9,8},{10,11... | collective-permute-start | bytes 786440 | tf_op jit(solution)/shard_map/ppermute | solution.py:25
  13.5 1.7 copy-start.2
  15.3 1.7 copy-start.3
  17.0 2.8 %copy-start.10 = (bf16[256,512]{1,0:T(8,128)(2,1)S(1)}, bf16[256,512]{1,0:T(8,128)(2,1)}, u32[]{:S(2)}) copy-start(bf16[256,512]{1,0:T(8,128)(2,1)} %copy-done.9) | copy-start | bytes 786436
  17.9 44.7 %collective-permute-start.7 = (bf16[4,1048,128]{2,1,0:T(8,128)(2,1)S(1)}, bf16[4,1048,128]{2,1,0:T(8,128)(2,1)S(1)}, u32[]{:S(2)}, u32[]{:S(2)}) collective-permute-start(bf16[4,1048,128]{2,1,0:T(8,128)(2,1)S(1)} %pack.8.refs_3_), channel_id=1, source_target_pairs={{2,0},{4,2},{6,4},{8,6},{10,8},{12,10},{14,12},{16,14},{18,16},{20... | collective-permute-start | bytes 3219464 | tf_op jit(solution)/shard_map/ppermute | solution.py:31
  19.8 10.1 %collective-permute-start.2 = (bf16[256,512]{1,0:T(8,128)(2,1)S(1)}, bf16[256,512]{1,0:T(8,128)(2,1)S(1)}, u32[]{:S(2)}, u32[]{:S(2)}) collective-permute-start(bf16[256,512]{1,0:T(8,128)(2,1)S(1)} %copy-done.10), channel_id=1, source_target_pairs={{0,1},{1,0},{2,3},{3,2},{4,5},{5,4},{6,7},{7,6},{8,9},{9,8},{10,11... | collective-permute-start | bytes 786440 | tf_op jit(solution)/shard_map/ppermute | solution.py:25
  20.4 17.6 %collective-permute-start.9 = (bf16[512,512]{1,0:T(8,128)(2,1)S(1)}, bf16[512,512]{1,0:T(8,128)(2,1)S(1)}, u32[]{:S(2)}, u32[]{:S(2)}) collective-permute-start(bf16[512,512]{1,0:T(8,128)(2,1)S(1)} %slice.4), channel_id=1, source_target_pairs={{2,0},{4,2},{6,4},{8,6},{10,8},{12,10},{14,12},{16,14},{18,16},{20... | collective-permute-start | bytes 1572872 | tf_op jit(solution)/shard_map/ppermute | solution.py:31
  22.5 12.4 %collective-permute-start = (bf16[256,512]{1,0:T(8,128)(2,1)S(1)}, bf16[256,512]{1,0:T(8,128)(2,1)S(1)}, u32[]{:S(2)}, u32[]{:S(2)}) collective-permute-start(bf16[256,512]{1,0:T(8,128)(2,1)S(1)} %get-tuple-element.38), channel_id=1, source_target_pairs={{0,1},{1,0},{2,3},{3,2},{4,5},{5,4},{6,7},{7,6},{8,9},{9,8},{10,11... | collective-permute-start | bytes 786440 | tf_op jit(solution)/shard_map/ppermute | solution.py:25
  25.2 44.6 %collective-permute-start.5 = (bf16[4,1048,128]{2,1,0:T(8,128)(2,1)S(1)}, bf16[4,1048,128]{2,1,0:T(8,128)(2,1)S(1)}, u32[]{:S(2)}, u32[]{:S(2)}) collective-permute-start(bf16[4,1048,128]{2,1,0:T(8,128)(2,1)S(1)} %pack.7.refs_3_), channel_id=1, source_target_pairs={{2,0},{4,2},{6,4},{8,6},{10,8},{12,10},{14,12},{16,14},{18,16},{20... | collective-permute-start | bytes 3219464 | tf_op jit(solution)/shard_map/ppermute | solution.py:31
  29.9 25.4 %collective-permute-start.10 = (bf16[4,536,128]{2,1,0:T(8,128)(2,1)S(1)}, bf16[4,536,128]{2,1,0:T(8,128)(2,1)S(1)}, u32[]{:S(2)}, u32[]{:S(2)}) collective-permute-start(bf16[4,536,128]{2,1,0:T(8,128)(2,1)S(1)} %pack.9.refs_3_), channel_id=1, source_target_pairs={{2,0},{4,2},{6,4},{8,6},{10,8},{12,10},{14,12},{16,14},{18,16},{20... | collective-permute-start | bytes 1646600 | tf_op jit(solution)/shard_map/ppermute | solution.py:31
  34.9 42.1 %collective-permute-start.3 = (bf16[4,1048,128]{2,1,0:T(8,128)(2,1)S(1)}, bf16[4,1048,128]{2,1,0:T(8,128)(2,1)S(1)}, u32[]{:S(2)}, u32[]{:S(2)}) collective-permute-start(bf16[4,1048,128]{2,1,0:T(8,128)(2,1)S(1)} %pack.6.refs_3_), channel_id=1, source_target_pairs={{2,0},{4,2},{6,4},{8,6},{10,8},{12,10},{14,12},{16,14},{18,16},{20... | collective-permute-start | bytes 3219464 | tf_op jit(solution)/shard_map/ppermute | solution.py:31
  36.8 18.6 %copy-start.4 = (bf16[1,512,2560]{2,1,0:T(8,128)(2,1)S(1)}, bf16[1,512,2560]{2,1,0:T(8,128)(2,1)}, u32[]{:S(2)}) copy-start(bf16[1,512,2560]{2,1,0:T(8,128)(2,1)} %param.9) | copy-start | bytes 7864324
  36.8 18.6 %copy-start.5 = (bf16[1,512,2560]{2,1,0:T(8,128)(2,1)S(1)}, bf16[1,512,2560]{2,1,0:T(8,128)(2,1)}, u32[]{:S(2)}) copy-start(bf16[1,512,2560]{2,1,0:T(8,128)(2,1)} %param.10) | copy-start | bytes 7864324
  36.8 18.6 %copy-start.7 = (s32[16]{0:T(128)S(1)}, s32[16]{0:T(128)}, u32[]{:S(2)}) copy-start(s32[16]{0:T(128)} %lengths.9) | copy-start | bytes 196
  36.8 18.5 %copy-start.8 = (s32[16]{0:T(128)S(1)}, s32[16]{0:T(128)}, u32[]{:S(2)}) copy-start(s32[16]{0:T(128)} %sources.9) | copy-start | bytes 196
  38.0 46.2 %collective-permute-start.1 = (bf16[4,1048,128]{2,1,0:T(8,128)(2,1)S(1)}, bf16[4,1048,128]{2,1,0:T(8,128)(2,1)S(1)}, u32[]{:S(2)}, u32[]{:S(2)}) collective-permute-start(bf16[4,1048,128]{2,1,0:T(8,128)(2,1)S(1)} %pack.5.refs_3_), channel_id=1, source_target_pairs={{2,0},{4,2},{6,4},{8,6},{10,8},{12,10},{14,12},{16,14},{18,16},{20... | collective-permute-start | bytes 3219464 | tf_op jit(solution)/shard_map/ppermute | solution.py:31
  91.6 34.4 %collective-permute-start.11 = (bf16[12,512,128]{2,1,0:T(8,128)(2,1)S(1)}, bf16[12,512,128]{2,1,0:T(8,128)(2,1)S(1)}, u32[]{:S(2)}, u32[]{:S(2)}) collective-permute-start(bf16[12,512,128]{2,1,0:T(8,128)(2,1)S(1)} %get-tuple-element.57), channel_id=1, source_target_pairs={{0,2},{2,4},{4,6},{6,8},{8,10},{10,12},{12,14},{14,16},{16,18},{18... | collective-permute-start | bytes 4718600 | tf_op jit(solution)/shard_map/ppermute | solution.py:31
  95.3 29.4 %collective-permute-start.12 = (bf16[8,512,128]{2,1,0:T(8,128)(2,1)S(1)}, bf16[8,512,128]{2,1,0:T(8,128)(2,1)S(1)}, u32[]{:S(2)}, u32[]{:S(2)}) collective-permute-start(bf16[8,512,128]{2,1,0:T(8,128)(2,1)S(1)} %get-tuple-element.59), channel_id=1, source_target_pairs={{0,2},{2,4},{4,6},{6,8},{8,10},{10,12},{12,14},{14,16},{16,18},{18... | collective-permute-start | bytes 3145736 | tf_op jit(solution)/shard_map/ppermute | solution.py:31
  97.3 32.8 %collective-permute-start.15 = (bf16[2,256,512]{2,1,0:T(8,128)(2,1)S(1)}, bf16[2,256,512]{2,1,0:T(8,128)(2,1)S(1)}, u32[]{:S(2)}, u32[]{:S(2)}) collective-permute-start(bf16[2,256,512]{2,1,0:T(8,128)(2,1)S(1)} %bitcast.67), channel_id=1, source_target_pairs={{0,1},{1,0},{2,3},{3,2},{4,5},{5,4},{6,7},{7,6},{8,9},{9,8},{10,11... | collective-permute-start | bytes 1572872 | tf_op jit(solution)/shard_map/ppermute | solution.py:25
  97.8 33.7 %collective-permute-start.19 = (bf16[2,256,512]{2,1,0:T(8,128)(2,1)S(1)}, bf16[2,256,512]{2,1,0:T(8,128)(2,1)S(1)}, u32[]{:S(2)}, u32[]{:S(2)}) collective-permute-start(bf16[2,256,512]{2,1,0:T(8,128)(2,1)S(1)} %bitcast.70), channel_id=1, source_target_pairs={{0,1},{1,0},{2,3},{3,2},{4,5},{5,4},{6,7},{7,6},{8,9},{9,8},{10,11... | collective-permute-start | bytes 1572872 | tf_op jit(solution)/shard_map/ppermute | solution.py:25
  127.4 64.4 %collective-permute-start.13 = (bf16[1,256,1536]{2,1,0:T(8,128)(2,1)S(1)}, bf16[1,256,1536]{2,1,0:T(8,128)(2,1)S(1)}, u32[]{:S(2)}, u32[]{:S(2)}) collective-permute-start(bf16[1,256,1536]{2,1,0:T(8,128)(2,1)S(1)} %get-tuple-element.61), channel_id=1, source_target_pairs={{0,1},{1,0},{2,3},{3,2},{4,5},{5,4},{6,7},{7,6},{8,9},{9,8},{10,11... | collective-permute-start | bytes 2359304 | tf_op jit(solution)/shard_map/ppermute | solution.py:25
  128.0 31.1 %collective-permute-start.18 = (bf16[2,256,512]{2,1,0:T(8,128)(2,1)S(1)}, bf16[2,256,512]{2,1,0:T(8,128)(2,1)S(1)}, u32[]{:S(2)}, u32[]{:S(2)}) collective-permute-start(bf16[2,256,512]{2,1,0:T(8,128)(2,1)S(1)} %bitcast.69), channel_id=1, source_target_pairs={{0,1},{1,0},{2,3},{3,2},{4,5},{5,4},{6,7},{7,6},{8,9},{9,8},{10,11... | collective-permute-start | bytes 1572872 | tf_op jit(solution)/shard_map/ppermute | solution.py:25
  129.5 40.9 %collective-permute-start.17 = (bf16[2,256,512]{2,1,0:T(8,128)(2,1)S(1)}, bf16[2,256,512]{2,1,0:T(8,128)(2,1)S(1)}, u32[]{:S(2)}, u32[]{:S(2)}) collective-permute-start(bf16[2,256,512]{2,1,0:T(8,128)(2,1)S(1)} %bitcast.68), channel_id=1, source_target_pairs={{0,1},{1,0},{2,3},{3,2},{4,5},{5,4},{6,7},{7,6},{8,9},{9,8},{10,11... | collective-permute-start | bytes 1572872 | tf_op jit(solution)/shard_map/ppermute | solution.py:25
  130.0 51.6 %collective-permute-start.16 = (bf16[2,256,512]{2,1,0:T(8,128)(2,1)S(1)}, bf16[2,256,512]{2,1,0:T(8,128)(2,1)S(1)}, u32[]{:S(2)}, u32[]{:S(2)}) collective-permute-start(bf16[2,256,512]{2,1,0:T(8,128)(2,1)S(1)} %bitcast.66), channel_id=1, source_target_pairs={{0,1},{1,0},{2,3},{3,2},{4,5},{5,4},{6,7},{7,6},{8,9},{9,8},{10,11... | collective-permute-start | bytes 1572872 | tf_op jit(solution)/shard_map/ppermute | solution.py:25
  131.5 59.5 %collective-permute-start.14 = (bf16[1,256,1024]{2,1,0:T(8,128)(2,1)S(1)}, bf16[1,256,1024]{2,1,0:T(8,128)(2,1)S(1)}, u32[]{:S(2)}, u32[]{:S(2)}) collective-permute-start(bf16[1,256,1024]{2,1,0:T(8,128)(2,1)S(1)} %get-tuple-element.62), channel_id=1, source_target_pairs={{0,1},{1,0},{2,3},{3,2},{4,5},{5,4},{6,7},{7,6},{8,9},{9,8},{10,11... | collective-permute-start | bytes 1572872 | tf_op jit(solution)/shard_map/ppermute | solution.py:25
where the time goes:
time: 193 us
  waiting for transfers between devices  106 us (55%)
  Pallas kernels  47.4 us (25%)
  starting transfers between devices  31 us (16%)
  local copies, waits for them, and re-layouts  7.1 us (4%)
    ppermute x12, waiting for transfers between devices, shifted(): lax.ppermute(block, axis, [(i, (i + distance) % size) for i in range(size)])  67.2 us
    ppermute x8, waiting for transfers between devices, passed_along(): return lax.ppermute(block, axis, route)  39.1 us
    pallas_call x5, Pallas kernels, grads(): pl.pallas_call(functools.partial(grads_kernel, carried=len(carried), tile...  36.2 us
    ppermute x8, starting transfers between devices, passed_along(): return lax.ppermute(block, axis, route)  19.4 us
    ppermute x12, starting transfers between devices, shifted(): lax.ppermute(block, axis, [(i, (i + distance) % size) for i in range(size)])  11.7 us
    unnamed x22, local copies, waits for them, and re-layouts  6.1 us
    pallas_call x5, Pallas kernels, pack(): pl.pallas_call(functools.partial(pack_kernel, first=first, joined=joined)...  4.41 us
  transfers between devices with their start and end apart: 20, of which 10 were waited for; matrix products, arithmetic and copies ran while one was open for 1% of the time, Pallas kernels for 20%

commit v1 on v0

--- a/solution.py
+++ b/solution.py
@@ -10,14 +10,14 @@
 
 
 HEAD_DIM = 128
-STAT_ROWS = 24
+STAT_ROWS = 32
 DEAD = 1e30
 LOG2E = 1.4426950408889634
-VMEM_LIMIT = 30 * 1024 * 1024
+VMEM_LIMIT = 24 * 1024 * 1024
 KEY_TILE = 512
 CHUNKS = (4, 4, 4, 4, 4)
 MOVES = ((0,),)
-GROUPS = ((0, 1), (2, 3, 4))
+GROUPS = ((0, 1, 2), (3, 4))
 
 
 def shifted(block, axis, distance):
@@ -136,8 +136,7 @@
             for part in parts
             for j in range(lanes)
         ]
-        if len(pieces) < STAT_ROWS:
-            pieces.append(jnp.zeros((STAT_ROWS - len(pieces), HEAD_DIM), jnp.float32))
+        pieces.append(jnp.zeros((STAT_ROWS - len(pieces), HEAD_DIM), jnp.float32))
         packed[h, top + rows :, :] = jnp.concatenate(pieces, axis=0).astype(jnp.bfloat16)
 
 
@@ -410,9 +409,10 @@
             num_scalar_prefetch=0,
             grid=(1,),
             in_specs=[
-                any_spec
-                for _ in (*blocks, *outs)
-            ],
+                pl.BlockSpec(b.shape, functools.partial(lambda n, i: (0,) * n, b.ndim))
+                for b in blocks
+            ]
+            + [any_spec] * len(outs),
             out_specs=[any_spec] * len(outs),
             scratch_shapes=[pltpu.SemaphoreType.DMA((copies,))],
         ),

time: 193 us -> 191 us (0.990)
  the two profiles are of different devices: /device:TPU:6 before, /device:TPU:0 now
where the time goes in v1:
time: 191 us
  waiting for transfers between devices  93.5 us (49%)
  Pallas kernels  47.2 us (25%)
  starting transfers between devices  42.7 us (22%)
  local copies, waits for them, and re-layouts  6.17 us (3%)
    ppermute x12, waiting for transfers between devices, shifted(): lax.ppermute(block, axis, [(i, (i + distance) % size) for i in range(size)])  93.4 us
    pallas_call x5, Pallas kernels, grads(): pl.pallas_call(functools.partial(grads_kernel, carried=len(carried), tile...  36 us
    ppermute x8, starting transfers between devices, passed_along(): return lax.ppermute(block, axis, route)  27.5 us
    ppermute x12, starting transfers between devices, shifted(): lax.ppermute(block, axis, [(i, (i + distance) % size) for i in range(size)])  15.2 us
    unnamed x24, local copies, waits for them, and re-layouts  6.1 us
    pallas_call x5, Pallas kernels, pack(): pl.pallas_call(functools.partial(pack_kernel, first=first, joined=joined)...  4.41 us
  transfers between devices with their start and end apart: 20, of which 10 were waited for; matrix products, arithmetic and copies ran while one was open for 0% of the time, Pallas kernels for 24%

profile of v1, /device:TPU:0, one launch (start us, length us, event | category | flops | bytes accessed | tf_op | source)
XLA Modules:
  0.0 190.7 jit_solution(7833079880589539621)
XLA Ops:
  0.7 1.9 copy-done.1
  2.5 0.9 cut.1
  3.5 0.7 copy-done.10
  4.2 3.0 %collective-permute-start.6 = (bf16[256,512]{1,0:T(8,128)(2,1)}, bf16[256,512]{1,0:T(8,128)(2,1)S(1)}, u32[]{:S(2)}, u32[]{:S(2)}) collective-permute-start(bf16[256,512]{1,0:T(8,128)(2,1)} %get-tuple-element.41), channel_id=1, source_target_pairs={{0,1},{1,0},{2,3},{3,2},{4,5},{5,4},{6,7},{7,6},{8,9},{9,8},{10,11... | collective-permute-start | bytes 786440 | tf_op jit(solution)/shard_map/ppermute | solution.py:25
  7.2 7.3 %collective-permute-done.6 = bf16[256,512]{1,0:T(8,128)(2,1)S(1)} collective-permute-done((bf16[256,512]{1,0:T(8,128)(2,1)}, bf16[256,512]{1,0:T(8,128)(2,1)S(1)}, u32[]{:S(2)}, u32[]{:S(2)}) %collective-permute-start.6) | collective-permute-done | bytes 262176 | tf_op jit(solution)/shard_map/ppermute | solution.py:25
  14.5 1.7 copy-done.2
  16.3 1.7 copy-done.3
  18.0 0.8 pack.8.refs_3_
  18.8 1.3 collective-permute-start.7
  20.2 2.1 %collective-permute-start.8 = (bf16[256,512]{1,0:T(8,128)(2,1)S(1)}, bf16[256,512]{1,0:T(8,128)(2,1)S(1)}, u32[]{:S(2)}, u32[]{:S(2)}) collective-permute-start(bf16[256,512]{1,0:T(8,128)(2,1)S(1)} %dynamic-slice_bitcast_fusion), channel_id=1, source_target_pairs={{0,1},{1,0},{2,3},{3,2},{4,5},{5,4},{6,7},{7,6},{8,9},{9,8},{10,11... | collective-permute-start | bytes 786440 | tf_op jit(solution)/shard_map/ppermute | solution.py:25
  22.3 0.8 pack.7.refs_3_
  23.1 1.3 collective-permute-start.5
  24.5 4.4 %collective-permute-done.8 = bf16[256,512]{1,0:T(8,128)(2,1)S(1)} collective-permute-done((bf16[256,512]{1,0:T(8,128)(2,1)S(1)}, bf16[256,512]{1,0:T(8,128)(2,1)S(1)}, u32[]{:S(2)}, u32[]{:S(2)}) %collective-permute-start.8) | collective-permute-done | bytes 262176 | tf_op jit(solution)/shard_map/ppermute | solution.py:25
  29.0 1.1 pack.9.refs_3_
  30.1 1.3 collective-permute-start.10
  31.4 1.3 collective-permute-start.9
  32.7 1.9 %collective-permute-done.2 = bf16[256,512]{1,0:T(8,128)(2,1)S(1)} collective-permute-done((bf16[256,512]{1,0:T(8,128)(2,1)S(1)}, bf16[256,512]{1,0:T(8,128)(2,1)S(1)}, u32[]{:S(2)}, u32[]{:S(2)}) %collective-permute-start.2) | collective-permute-done | bytes 262176 | tf_op jit(solution)/shard_map/ppermute | solution.py:25
  34.6 2.3 %collective-permute-start = (bf16[256,512]{1,0:T(8,128)(2,1)S(1)}, bf16[256,512]{1,0:T(8,128)(2,1)S(1)}, u32[]{:S(2)}, u32[]{:S(2)}) collective-permute-start(bf16[256,512]{1,0:T(8,128)(2,1)S(1)} %get-tuple-element.38), channel_id=1, source_target_pairs={{0,1},{1,0},{2,3},{3,2},{4,5},{5,4},{6,7},{7,6},{8,9},{9,8},{10,11... | collective-permute-start | bytes 786440 | tf_op jit(solution)/shard_map/ppermute | solution.py:25
  36.9 0.8 pack.6.refs_3_
  37.7 5.8 %collective-permute-done = bf16[256,512]{1,0:T(8,128)(2,1)S(1)} collective-permute-done((bf16[256,512]{1,0:T(8,128)(2,1)S(1)}, bf16[256,512]{1,0:T(8,128)(2,1)S(1)}, u32[]{:S(2)}, u32[]{:S(2)}) %collective-permute-start) | collective-permute-done | bytes 262176 | tf_op jit(solution)/shard_map/ppermute | solution.py:25
  43.5 1.3 collective-permute-start.3
  44.8 0.9 pack.5.refs_3_
  45.7 1.6 collective-permute-start.1
  47.4 7.2 %grads.5 = (bf16[256,5120]{1,0:T(8,128)(2,1)}, bf16[256,5120]{1,0:T(8,128)(2,1)}, bf16[1,2,256,512]{3,2,1,0:T(8,128)(2,1)S(1)}, f32[12,512,128]{2,1,0:T(8,128)S(1)}, bf16[12,512,128]{2,1,0:T(8,128)(2,1)S(1)}) custom-call(s32[16]{0:T(128)S(1)} %copy-done.8, s32[16]{0:T(128)S(1)} %copy-done.9, bf16[512,2560]{1,0:T(8,128)(2,1)S(1)} %bitcast.46, ...), custom_call_target="tpu_custom_call" | custom-call | flops 2684354560 | bytes 6291456 | tf_op jit(solution)/shard_map/grads/pallas_call | solution.py:274
  54.6 7.2 %grads.6 = (bf16[256,5120]{1,0:T(8,128)(2,1)}, bf16[256,5120]{1,0:T(8,128)(2,1)}, bf16[1,2,256,512]{3,2,1,0:T(8,128)(2,1)S(1)}, f32[12,512,128]{2,1,0:T(8,128)S(1)}, bf16[12,512,128]{2,1,0:T(8,128)(2,1)S(1)}) custom-call(s32[16]{0:T(128)S(1)} %copy-done.8, ...), custom_call_target="tpu_custom_call", output_to_operand_aliasing={{0}: (8, {}), {1}: (9, {}), {3}: (10, {}), {4}: (11, {})} | custom-call | flops 2684354560 | bytes 6291456 | tf_op jit(solution)/shard_map/grads/pallas_call | solution.py:274
  61.8 7.2 %grads.7 = (bf16[256,5120]{1,0:T(8,128)(2,1)}, bf16[256,5120]{1,0:T(8,128)(2,1)}, bf16[1,2,256,512]{3,2,1,0:T(8,128)(2,1)S(1)}, f32[12,512,128]{2,1,0:T(8,128)S(1)}, bf16[12,512,128]{2,1,0:T(8,128)(2,1)S(1)}) custom-call(s32[16]{0:T(128)S(1)} %copy-done.8, ...), custom_call_target="tpu_custom_call", output_to_operand_aliasing={{0}: (8, {}), {1}: (9, {}), {3}: (10, {}), {4}: (11, {})} | custom-call | flops 2684354560 | bytes 6291456 | tf_op jit(solution)/shard_map/grads/pallas_call | solution.py:274
  69.0 15.8 %collective-permute-start.12 = (bf16[12,512,128]{2,1,0:T(8,128)(2,1)S(1)}, bf16[12,512,128]{2,1,0:T(8,128)(2,1)S(1)}, u32[]{:S(2)}, u32[]{:S(2)}) collective-permute-start(bf16[12,512,128]{2,1,0:T(8,128)(2,1)S(1)} %get-tuple-element.59), channel_id=1, source_target_pairs={{0,2},{2,4},{4,6},{6,8},{8,10},{10,12},{12,14},{14,16},{16,18},{18... | collective-permute-start | bytes 4718600 | tf_op jit(solution)/shard_map/ppermute | solution.py:31
  84.9 7.2 %grads.8 = (bf16[256,5120]{1,0:T(8,128)(2,1)}, bf16[256,5120]{1,0:T(8,128)(2,1)}, bf16[1,2,256,512]{3,2,1,0:T(8,128)(2,1)S(1)}, f32[8,512,128]{2,1,0:T(8,128)S(1)}, bf16[8,512,128]{2,1,0:T(8,128)(2,1)S(1)}) custom-call(s32[16]{0:T(128)S(1)} %copy-done.8, s32[16]{0:T(128)S(1)} %copy-done.9, ...), custom_call_target="tpu_custom_call", output_to_operand_aliasing={{0}: (8, {}), {1}: (9, {})} | custom-call | flops 2684354560 | bytes 6291456 | tf_op jit(solution)/shard_map/grads/pallas_call | solution.py:274
  92.1 7.2 %grads.9 = (bf16[256,5120]{1,0:T(8,128)(2,1)}, bf16[256,5120]{1,0:T(8,128)(2,1)}, bf16[1,2,256,512]{3,2,1,0:T(8,128)(2,1)S(1)}, f32[8,512,128]{2,1,0:T(8,128)S(1)}, bf16[8,512,128]{2,1,0:T(8,128)(2,1)S(1)}) custom-call(s32[16]{0:T(128)S(1)} %copy-done.8, s32[16]{0:T(128)S(1)} %copy-done.9, ...), custom_call_target="tpu_custom_call", output_to_operand_aliasing={{0}: (8, {}), {1}: (9, {}), {3}: (10, {}), {4}: (11, {})} | custom-call | flops 2684354560 | bytes 6291456 | tf_op jit(solution)/shard_map/grads/pallas_call | solution.py:274
  99.2 3.6 %collective-permute-start.11 = (bf16[8,512,128]{2,1,0:T(8,128)(2,1)S(1)}, bf16[8,512,128]{2,1,0:T(8,128)(2,1)S(1)}, u32[]{:S(2)}, u32[]{:S(2)}) collective-permute-start(bf16[8,512,128]{2,1,0:T(8,128)(2,1)S(1)} %get-tuple-element.57), channel_id=1, source_target_pairs={{0,2},{2,4},{4,6},{6,8},{8,10},{10,12},{12,14},{14,16},{16,18},{18... | collective-permute-start | bytes 3145736 | tf_op jit(solution)/shard_map/ppermute | solution.py:31
  102.8 1.6 collective-permute-start.15
  104.4 0.5 collective-permute-start.19
  104.9 1.4 query_sum.2
  106.3 1.6 collective-permute-start.14
  107.9 0.5 collective-permute-start.18
  108.4 9.3 %collective-permute-done.15.refs_0_ = bf16[2,256,512]{2,1,0:T(8,128)(2,1)S(1)} collective-permute-done((bf16[2,256,512]{2,1,0:T(8,128)(2,1)S(1)}, bf16[2,256,512]{2,1,0:T(8,128)(2,1)S(1)}, u32[]{:S(2)}, u32[]{:S(2)}) %collective-permute-start.15) | collective-permute-done | bytes 524320 | tf_op jit(solution)/shard_map/ppermute | solution.py:25
  117.7 1.5 collective-permute-start.17
  119.2 0.5 collective-permute-start.16
  119.7 1.3 query_sum.3
  121.0 7.9 %collective-permute-done.19.refs_4_ = bf16[2,256,512]{2,1,0:T(8,128)(2,1)S(1)} collective-permute-done((bf16[2,256,512]{2,1,0:T(8,128)(2,1)S(1)}, bf16[2,256,512]{2,1,0:T(8,128)(2,1)S(1)}, u32[]{:S(2)}, u32[]{:S(2)}) %collective-permute-start.19) | collective-permute-done | bytes 524320 | tf_op jit(solution)/shard_map/ppermute | solution.py:25
  128.9 1.5 collective-permute-start.13
  130.4 26.6 %collective-permute-done.18.refs_3_ = bf16[2,256,512]{2,1,0:T(8,128)(2,1)S(1)} collective-permute-done((bf16[2,256,512]{2,1,0:T(8,128)(2,1)S(1)}, bf16[2,256,512]{2,1,0:T(8,128)(2,1)S(1)}, u32[]{:S(2)}, u32[]{:S(2)}) %collective-permute-start.18) | collective-permute-done | bytes 524320 | tf_op jit(solution)/shard_map/ppermute | solution.py:25
  157.0 11.2 %collective-permute-done.17.refs_2_ = bf16[2,256,512]{2,1,0:T(8,128)(2,1)S(1)} collective-permute-done((bf16[2,256,512]{2,1,0:T(8,128)(2,1)S(1)}, bf16[2,256,512]{2,1,0:T(8,128)(2,1)S(1)}, u32[]{:S(2)}, u32[]{:S(2)}) %collective-permute-start.17) | collective-permute-done | bytes 524320 | tf_op jit(solution)/shard_map/ppermute | solution.py:25
  168.3 11.2 %collective-permute-done.16.refs_1_ = bf16[2,256,512]{2,1,0:T(8,128)(2,1)S(1)} collective-permute-done((bf16[2,256,512]{2,1,0:T(8,128)(2,1)S(1)}, bf16[2,256,512]{2,1,0:T(8,128)(2,1)S(1)}, u32[]{:S(2)}, u32[]{:S(2)}) %collective-permute-start.16) | collective-permute-done | bytes 524320 | tf_op jit(solution)/shard_map/ppermute | solution.py:25
  179.5 1.6 place.5
  181.1 0.9 place.3.refs_1_
  182.0 7.7 %collective-permute-done.13.refs_0_ = bf16[1,256,1024]{2,1,0:T(8,128)(2,1)S(1)} collective-permute-done((bf16[1,256,1024]{2,1,0:T(8,128)(2,1)S(1)}, bf16[1,256,1024]{2,1,0:T(8,128)(2,1)S(1)}, u32[]{:S(2)}, u32[]{:S(2)}) %collective-permute-start.13) | collective-permute-done | bytes 524320 | tf_op jit(solution)/shard_map/ppermute | solution.py:25
  189.7 0.8 place.4
  (34 shorter events, 0.3 us)
Async XLA Ops:
  0.6 13.9 %copy-start = (bf16[1,512,2560]{2,1,0:T(8,128)(2,1)S(1)}, bf16[1,512,2560]{2,1,0:T(8,128)(2,1)}, u32[]{:S(2)}) copy-start(bf16[1,512,2560]{2,1,0:T(8,128)(2,1)} %param.8) | copy-start | bytes 7864324
  0.6 1.9 copy-start.1
  2.5 12.0 %copy-start.7 = (f32[1,20,512]{2,0,1:T(1,128)S(1)}, f32[1,20,512]{2,0,1:T(1,128)}, u32[]{:S(2)}) copy-start(f32[1,20,512]{2,0,1:T(1,128)} %param.13) | copy-start | bytes 122884
  3.4 0.7 copy-start.10
  4.2 10.4 %collective-permute-start.6 = (bf16[256,512]{1,0:T(8,128)(2,1)}, bf16[256,512]{1,0:T(8,128)(2,1)S(1)}, u32[]{:S(2)}, u32[]{:S(2)}) collective-permute-start(bf16[256,512]{1,0:T(8,128)(2,1)} %get-tuple-element.41), channel_id=1, source_target_pairs={{0,1},{1,0},{2,3},{3,2},{4,5},{5,4},{6,7},{7,6},{8,9},{9,8},{10,11... | collective-permute-start | bytes 786440 | tf_op jit(solution)/shard_map/ppermute | solution.py:25
  7.1 15.1 %collective-permute-start.4 = (bf16[256,512]{1,0:T(8,128)(2,1)}, bf16[256,512]{1,0:T(8,128)(2,1)S(1)}, u32[]{:S(2)}, u32[]{:S(2)}) collective-permute-start(bf16[256,512]{1,0:T(8,128)(2,1)} %get-tuple-element.40), channel_id=1, source_target_pairs={{0,1},{1,0},{2,3},{3,2},{4,5},{5,4},{6,7},{7,6},{8,9},{9,8},{10,11... | collective-permute-start | bytes 786440 | tf_op jit(solution)/shard_map/ppermute | solution.py:25
  14.5 1.7 copy-start.2
  16.3 1.7 copy-start.3
  18.8 35.8 %collective-permute-start.7 = (bf16[4,1056,128]{2,1,0:T(8,128)(2,1)S(1)}, bf16[4,1056,128]{2,1,0:T(8,128)(2,1)S(1)}, u32[]{:S(2)}, u32[]{:S(2)}) collective-permute-start(bf16[4,1056,128]{2,1,0:T(8,128)(2,1)S(1)} %pack.8.refs_3_), channel_id=1, source_target_pairs={{2,0},{4,2},{6,4},{8,6},{10,8},{12,10},{14,12},{16,14},{18,16},{20... | collective-permute-start | bytes 3244040 | tf_op jit(solution)/shard_map/ppermute | solution.py:31
  20.2 8.8 %collective-permute-start.8 = (bf16[256,512]{1,0:T(8,128)(2,1)S(1)}, bf16[256,512]{1,0:T(8,128)(2,1)S(1)}, u32[]{:S(2)}, u32[]{:S(2)}) collective-permute-start(bf16[256,512]{1,0:T(8,128)(2,1)S(1)} %dynamic-slice_bitcast_fusion), channel_id=1, source_target_pairs={{0,1},{1,0},{2,3},{3,2},{4,5},{5,4},{6,7},{7,6},{8,9},{9,8},{10,11... | collective-permute-start | bytes 786440 | tf_op jit(solution)/shard_map/ppermute | solution.py:25
  22.3 2.2 %copy-start.11 = (bf16[256,512]{1,0:T(8,128)(2,1)S(1)}, bf16[256,512]{1,0:T(8,128)(2,1)}, u32[]{:S(2)}) copy-start(bf16[256,512]{1,0:T(8,128)(2,1)} %copy-done.10) | copy-start | bytes 786436
  23.1 38.7 %collective-permute-start.5 = (bf16[4,1056,128]{2,1,0:T(8,128)(2,1)S(1)}, bf16[4,1056,128]{2,1,0:T(8,128)(2,1)S(1)}, u32[]{:S(2)}, u32[]{:S(2)}) collective-permute-start(bf16[4,1056,128]{2,1,0:T(8,128)(2,1)S(1)} %pack.7.refs_3_), channel_id=1, source_target_pairs={{2,0},{4,2},{6,4},{8,6},{10,8},{12,10},{14,12},{16,14},{18,16},{20... | collective-permute-start | bytes 3244040 | tf_op jit(solution)/shard_map/ppermute | solution.py:31
  24.4 10.2 %collective-permute-start.2 = (bf16[256,512]{1,0:T(8,128)(2,1)S(1)}, bf16[256,512]{1,0:T(8,128)(2,1)S(1)}, u32[]{:S(2)}, u32[]{:S(2)}) collective-permute-start(bf16[256,512]{1,0:T(8,128)(2,1)S(1)} %copy-done.11), channel_id=1, source_target_pairs={{0,1},{1,0},{2,3},{3,2},{4,5},{5,4},{6,7},{7,6},{8,9},{9,8},{10,11... | collective-permute-start | bytes 786440 | tf_op jit(solution)/shard_map/ppermute | solution.py:25
  30.1 17.3 %collective-permute-start.10 = (bf16[4,544,128]{2,1,0:T(8,128)(2,1)S(1)}, bf16[4,544,128]{2,1,0:T(8,128)(2,1)S(1)}, u32[]{:S(2)}, u32[]{:S(2)}) collective-permute-start(bf16[4,544,128]{2,1,0:T(8,128)(2,1)S(1)} %pack.9.refs_3_), channel_id=1, source_target_pairs={{2,0},{4,2},{6,4},{8,6},{10,8},{12,10},{14,12},{16,14},{18,16},{20... | collective-permute-start | bytes 1671176 | tf_op jit(solution)/shard_map/ppermute | solution.py:31
  31.4 14.3 %collective-permute-start.9 = (bf16[512,512]{1,0:T(8,128)(2,1)S(1)}, bf16[512,512]{1,0:T(8,128)(2,1)S(1)}, u32[]{:S(2)}, u32[]{:S(2)}) collective-permute-start(bf16[512,512]{1,0:T(8,128)(2,1)S(1)} %slice.4), channel_id=1, source_target_pairs={{2,0},{4,2},{6,4},{8,6},{10,8},{12,10},{14,12},{16,14},{18,16},{20... | collective-permute-start | bytes 1572872 | tf_op jit(solution)/shard_map/ppermute | solution.py:31
  34.6 8.9 %collective-permute-start = (bf16[256,512]{1,0:T(8,128)(2,1)S(1)}, bf16[256,512]{1,0:T(8,128)(2,1)S(1)}, u32[]{:S(2)}, u32[]{:S(2)}) collective-permute-start(bf16[256,512]{1,0:T(8,128)(2,1)S(1)} %get-tuple-element.38), channel_id=1, source_target_pairs={{0,1},{1,0},{2,3},{3,2},{4,5},{5,4},{6,7},{7,6},{8,9},{9,8},{10,11... | collective-permute-start | bytes 786440 | tf_op jit(solution)/shard_map/ppermute | solution.py:25
  36.9 7.9 %copy-start.4 = (bf16[1,512,2560]{2,1,0:T(8,128)(2,1)S(1)}, bf16[1,512,2560]{2,1,0:T(8,128)(2,1)}, u32[]{:S(2)}) copy-start(bf16[1,512,2560]{2,1,0:T(8,128)(2,1)} %param.11) | copy-start | bytes 7864324
  43.5 41.4 %collective-permute-start.3 = (bf16[4,1056,128]{2,1,0:T(8,128)(2,1)S(1)}, bf16[4,1056,128]{2,1,0:T(8,128)(2,1)S(1)}, u32[]{:S(2)}, u32[]{:S(2)}) collective-permute-start(bf16[4,1056,128]{2,1,0:T(8,128)(2,1)S(1)} %pack.6.refs_3_), channel_id=1, source_target_pairs={{2,0},{4,2},{6,4},{8,6},{10,8},{12,10},{14,12},{16,14},{18,16},{20... | collective-permute-start | bytes 3244040 | tf_op jit(solution)/shard_map/ppermute | solution.py:31
  44.8 2.5 %copy-start.5 = (bf16[1,512,2560]{2,1,0:T(8,128)(2,1)S(1)}, bf16[1,512,2560]{2,1,0:T(8,128)(2,1)}, u32[]{:S(2)}) copy-start(bf16[1,512,2560]{2,1,0:T(8,128)(2,1)} %param.9) | copy-start | bytes 7864324
  44.8 2.5 %copy-start.6 = (bf16[1,512,2560]{2,1,0:T(8,128)(2,1)S(1)}, bf16[1,512,2560]{2,1,0:T(8,128)(2,1)}, u32[]{:S(2)}) copy-start(bf16[1,512,2560]{2,1,0:T(8,128)(2,1)} %param.10) | copy-start | bytes 7864324
  44.8 2.5 %copy-start.8 = (s32[16]{0:T(128)S(1)}, s32[16]{0:T(128)}, u32[]{:S(2)}) copy-start(s32[16]{0:T(128)} %lengths.9) | copy-start | bytes 196
  44.8 2.5 %copy-start.9 = (s32[16]{0:T(128)S(1)}, s32[16]{0:T(128)}, u32[]{:S(2)}) copy-start(s32[16]{0:T(128)} %sources.9) | copy-start | bytes 196
  45.7 46.3 %collective-permute-start.1 = (bf16[4,1056,128]{2,1,0:T(8,128)(2,1)S(1)}, bf16[4,1056,128]{2,1,0:T(8,128)(2,1)S(1)}, u32[]{:S(2)}, u32[]{:S(2)}) collective-permute-start(bf16[4,1056,128]{2,1,0:T(8,128)(2,1)S(1)} %pack.5.refs_3_), channel_id=1, source_target_pairs={{2,0},{4,2},{6,4},{8,6},{10,8},{12,10},{14,12},{16,14},{18,16},{20... | collective-permute-start | bytes 3244040 | tf_op jit(solution)/shard_map/ppermute | solution.py:31
  69.0 35.9 %collective-permute-start.12 = (bf16[12,512,128]{2,1,0:T(8,128)(2,1)S(1)}, bf16[12,512,128]{2,1,0:T(8,128)(2,1)S(1)}, u32[]{:S(2)}, u32[]{:S(2)}) collective-permute-start(bf16[12,512,128]{2,1,0:T(8,128)(2,1)S(1)} %get-tuple-element.59), channel_id=1, source_target_pairs={{0,2},{2,4},{4,6},{6,8},{8,10},{10,12},{12,14},{14,16},{16,18},{18... | collective-permute-start | bytes 4718600 | tf_op jit(solution)/shard_map/ppermute | solution.py:31
  99.2 20.0 %collective-permute-start.11 = (bf16[8,512,128]{2,1,0:T(8,128)(2,1)S(1)}, bf16[8,512,128]{2,1,0:T(8,128)(2,1)S(1)}, u32[]{:S(2)}, u32[]{:S(2)}) collective-permute-start(bf16[8,512,128]{2,1,0:T(8,128)(2,1)S(1)} %get-tuple-element.57), channel_id=1, source_target_pairs={{0,2},{2,4},{4,6},{6,8},{8,10},{10,12},{12,14},{14,16},{16,18},{18... | collective-permute-start | bytes 3145736 | tf_op jit(solution)/shard_map/ppermute | solution.py:31
  102.8 14.9 %collective-permute-start.15 = (bf16[2,256,512]{2,1,0:T(8,128)(2,1)S(1)}, bf16[2,256,512]{2,1,0:T(8,128)(2,1)S(1)}, u32[]{:S(2)}, u32[]{:S(2)}) collective-permute-start(bf16[2,256,512]{2,1,0:T(8,128)(2,1)S(1)} %bitcast.68), channel_id=1, source_target_pairs={{0,1},{1,0},{2,3},{3,2},{4,5},{5,4},{6,7},{7,6},{8,9},{9,8},{10,11... | collective-permute-start | bytes 1572872 | tf_op jit(solution)/shard_map/ppermute | solution.py:25
  104.4 24.5 %collective-permute-start.19 = (bf16[2,256,512]{2,1,0:T(8,128)(2,1)S(1)}, bf16[2,256,512]{2,1,0:T(8,128)(2,1)S(1)}, u32[]{:S(2)}, u32[]{:S(2)}) collective-permute-start(bf16[2,256,512]{2,1,0:T(8,128)(2,1)S(1)} %bitcast.70), channel_id=1, source_target_pairs={{0,1},{1,0},{2,3},{3,2},{4,5},{5,4},{6,7},{7,6},{8,9},{9,8},{10,11... | collective-permute-start | bytes 1572872 | tf_op jit(solution)/shard_map/ppermute | solution.py:25
  106.3 74.7 %collective-permute-start.14 = (bf16[1,256,1536]{2,1,0:T(8,128)(2,1)S(1)}, bf16[1,256,1536]{2,1,0:T(8,128)(2,1)S(1)}, u32[]{:S(2)}, u32[]{:S(2)}) collective-permute-start(bf16[1,256,1536]{2,1,0:T(8,128)(2,1)S(1)} %get-tuple-element.62), channel_id=1, source_target_pairs={{0,1},{1,0},{2,3},{3,2},{4,5},{5,4},{6,7},{7,6},{8,9},{9,8},{10,11... | collective-permute-start | bytes 2359304 | tf_op jit(solution)/shard_map/ppermute | solution.py:25
  107.9 49.1 %collective-permute-start.18 = (bf16[2,256,512]{2,1,0:T(8,128)(2,1)S(1)}, bf16[2,256,512]{2,1,0:T(8,128)(2,1)S(1)}, u32[]{:S(2)}, u32[]{:S(2)}) collective-permute-start(bf16[2,256,512]{2,1,0:T(8,128)(2,1)S(1)} %bitcast.69), channel_id=1, source_target_pairs={{0,1},{1,0},{2,3},{3,2},{4,5},{5,4},{6,7},{7,6},{8,9},{9,8},{10,11... | collective-permute-start | bytes 1572872 | tf_op jit(solution)/shard_map/ppermute | solution.py:25
  117.7 50.6 %collective-permute-start.17 = (bf16[2,256,512]{2,1,0:T(8,128)(2,1)S(1)}, bf16[2,256,512]{2,1,0:T(8,128)(2,1)S(1)}, u32[]{:S(2)}, u32[]{:S(2)}) collective-permute-start(bf16[2,256,512]{2,1,0:T(8,128)(2,1)S(1)} %bitcast.67), channel_id=1, source_target_pairs={{0,1},{1,0},{2,3},{3,2},{4,5},{5,4},{6,7},{7,6},{8,9},{9,8},{10,11... | collective-permute-start | bytes 1572872 | tf_op jit(solution)/shard_map/ppermute | solution.py:25
  119.2 60.3 %collective-permute-start.16 = (bf16[2,256,512]{2,1,0:T(8,128)(2,1)S(1)}, bf16[2,256,512]{2,1,0:T(8,128)(2,1)S(1)}, u32[]{:S(2)}, u32[]{:S(2)}) collective-permute-start(bf16[2,256,512]{2,1,0:T(8,128)(2,1)S(1)} %bitcast.66), channel_id=1, source_target_pairs={{0,1},{1,0},{2,3},{3,2},{4,5},{5,4},{6,7},{7,6},{8,9},{9,8},{10,11... | collective-permute-start | bytes 1572872 | tf_op jit(solution)/shard_map/ppermute | solution.py:25
  128.9 60.8 %collective-permute-start.13 = (bf16[1,256,1024]{2,1,0:T(8,128)(2,1)S(1)}, bf16[1,256,1024]{2,1,0:T(8,128)(2,1)S(1)}, u32[]{:S(2)}, u32[]{:S(2)}) collective-permute-start(bf16[1,256,1024]{2,1,0:T(8,128)(2,1)S(1)} %get-tuple-element.61), channel_id=1, source_target_pairs={{0,1},{1,0},{2,3},{3,2},{4,5},{5,4},{6,7},{7,6},{8,9},{9,8},{10,11... | collective-permute-start | bytes 1572872 | tf_op jit(solution)/shard_map/ppermute | solution.py:25
